TPU v7x, 32 devices: a whole 2x2x4 slice. The times are simulated.
32 devices in a mesh: grp: 2 (over core), ctx: 4 (over z), wsh: 4 (over y, x).
Axes of the slice: x: 2, y: 2, z: 4, core: 2. Of those that a mesh axis runs over, the one named last changes fastest.
Arguments:
- tokens: bfloat16 [6144, 1152], P(('grp', 'ctx', 'wsh')), may hold values from -6 to 6
- segment_ids: int32 [6144], P(('grp', 'ctx', 'wsh')), may hold values from 0 to 1, as said below
- positions: int32 [6144], P(('grp', 'ctx', 'wsh')), may hold values from 0 to 3071, as said below
- attend_gain: float32 [1152], replicated, may hold values from 0.5 to 1.5
- query_key_value: bfloat16 [1152, 1920], P('wsh'), may hold values from -0.25 to 0.25
- attend_out: bfloat16 [1152, 1152], P('wsh'), may hold values from -2 to 2
- feed_gain: float32 [1152], replicated, may hold values from 0.5 to 1.5
- gate_up: bfloat16 [1152, 6144], P('wsh'), may hold values from -0.1875 to 0.1875
- down_weight: bfloat16 [3072, 1152], P('wsh'), may hold values from -0.4375 to 0.4375
- upstream: bfloat16 [6144, 1152], P(('grp', 'ctx', 'wsh')), may hold values from -6 to 6
Outputs:
- activations: bfloat16 [6144, 1152], P(('grp', 'ctx', 'wsh'))
- input_grad: float32 [6144, 1152], P(('grp', 'ctx', 'wsh'))
- query_key_value_grad: float32 [1152, 1920], P(('ctx', 'wsh'))
- attend_out_grad: float32 [1152, 1152], P(('ctx', 'wsh'))
- gate_up_grad: float32 [1152, 6144], P(('ctx', 'wsh'))
- down_weight_grad: float32 [3072, 1152], P(('ctx', 'wsh'))
- attend_gain_grad: float32 [1152], P(('ctx', 'wsh'))
- feed_gain_grad: float32 [1152], P(('ctx', 'wsh'))
Inputs may be any that keep to these rules, and one draw needn't show every extreme that they name: `segment_ids`: in each group of 3072 rows the aligned runs of 96 rows are the runs of 96 consecutive tokens of that group's token stream, in some order, each once; the stream is the prompt of 2048 tokens (segment 0) followed by 1 continuations of 1024 tokens (segments 1 to 1). `positions`: matching segment_ids: a prompt token's position is its index in the prompt; a continuation token's position is 2048 plus its index in its continuation.
All inputs are finite; a program needn't handle non-finite values.
Results may differ from a plain program's by a relative error of at most 0.02.
Values may be sent and summed in bfloat16 or wider, within the bound.
A program may use at most 256 MiB of HBM per device.

v0:
```python
import math
import jax
import jax.numpy as jnp
from jax import lax
from jax.sharding import PartitionSpec as P

HEADS = 18
KV_HEADS = 6
HEAD_DIM = 64
FF = 3072
KTILE = 1024
QW = 1152
KW = 384
EPSILON = 1e-05


def rope_angles(positions):
    halfway = HEAD_DIM // 2
    frequency = jnp.exp(jnp.arange(halfway, dtype=jnp.float32) * (-math.log(10000.0) / halfway))
    angles = positions.astype(jnp.float32)[:, None] * frequency[None, :]
    return (jnp.cos(angles), jnp.sin(angles))


def rotate(tensor, cosine, sine_table):
    halfway = tensor.shape[-1] // 2
    first_half = tensor[..., :halfway]
    second_half = tensor[..., halfway:]
    cos_wide = cosine[:, None, :]
    sin_wide = sine_table[:, None, :]
    return jnp.concatenate(
        [
            first_half * cos_wide - second_half * sin_wide,
            second_half * cos_wide + first_half * sin_wide,
        ],
        axis=-1,
    )


def unrotate(gradient, cosine, sine_table):
    halfway = gradient.shape[-1] // 2
    first_half = gradient[..., :halfway]
    second_half = gradient[..., halfway:]
    cos_wide = cosine[:, None, :]
    sin_wide = sine_table[:, None, :]
    return jnp.concatenate(
        [
            first_half * cos_wide + second_half * sin_wide,
            second_half * cos_wide - first_half * sin_wide,
        ],
        axis=-1,
    )


def rms_factor(values):
    return lax.rsqrt(jnp.mean(values * values, axis=-1, keepdims=True) + EPSILON)


def norm_back(grad_normed, inputs, factor, gain):
    weighted = grad_normed * gain
    inner_mean = jnp.mean(weighted * inputs, axis=-1, keepdims=True)
    input_part = factor * weighted - inputs * (factor * factor * factor) * inner_mean
    return (input_part, jnp.sum(grad_normed * inputs * factor, axis=0))


def rounded(values):
    return lax.optimization_barrier(values.astype(jnp.bfloat16)).astype(jnp.float32)


def tile_mask(segment_ids, positions, seg_key, pos_key):
    return (pos_key[None, :] <= positions[:, None]) & (
        (seg_key[None, :] == 0) | (seg_key[None, :] == segment_ids[:, None])
    )


def tile_scores(queries, key_tile, allowed):
    raw_scores = jnp.einsum(
        "nhjd,khd->hjnk", queries, key_tile, preferred_element_type=jnp.float32
    ) * HEAD_DIM ** (-0.5)
    return jnp.where(allowed, raw_scores, -1e30)


def split_tiles(key_all, value_all, seg_all, pos_all):
    tile_count = key_all.shape[0] // KTILE
    key_tiles = key_all.reshape(tile_count, KTILE, KV_HEADS, HEAD_DIM)
    value_tiles = value_all.reshape(tile_count, KTILE, KV_HEADS, HEAD_DIM)
    return (
        key_tiles,
        value_tiles,
        seg_all.reshape(tile_count, KTILE),
        pos_all.reshape(tile_count, KTILE),
    )


def attend_forward(queries, key_all, value_all, seg_all, pos_all, segment_ids, positions):
    local_rows = queries.shape[0]
    head_ratio = HEADS // KV_HEADS
    key_tiles, value_tiles, seg_tiles, pos_tiles = split_tiles(key_all, value_all, seg_all, pos_all)

    def stats_step(state_pair, pieces):
        running_max, running_sum = state_pair
        key_tile, seg_key, pos_key = pieces
        allowed = tile_mask(segment_ids, positions, seg_key, pos_key)
        scores = tile_scores(queries, key_tile, allowed)
        new_max = jnp.maximum(running_max, jnp.max(scores, axis=-1))
        expons = jnp.where(allowed, jnp.exp(scores - new_max[..., None]), 0.0)
        new_sum = running_sum * jnp.exp(running_max - new_max) + jnp.sum(expons, axis=-1)
        return ((new_max, new_sum), None)

    start_max = jnp.full((KV_HEADS, head_ratio, local_rows), -1e30, jnp.float32)
    start_sum = jnp.zeros((KV_HEADS, head_ratio, local_rows), jnp.float32)
    (row_max, row_sum), _ = lax.scan(
        stats_step, (start_max, start_sum), (key_tiles, seg_tiles, pos_tiles)
    )
    log_total = row_max + jnp.log(row_sum)

    def value_step(running, pieces):
        key_tile, value_tile, seg_key, pos_key = pieces
        allowed = tile_mask(segment_ids, positions, seg_key, pos_key)
        scores = tile_scores(queries, key_tile, allowed)
        weights_tile = jnp.where(allowed, jnp.exp(scores - log_total[..., None]), 0.0).astype(
            jnp.bfloat16
        )
        return (
            running
            + jnp.einsum(
                "hjnk,khd->nhjd", weights_tile, value_tile, preferred_element_type=jnp.float32
            ),
            None,
        )

    start_out = jnp.zeros((local_rows, KV_HEADS, head_ratio, HEAD_DIM), jnp.float32)
    output, _ = lax.scan(value_step, start_out, (key_tiles, value_tiles, seg_tiles, pos_tiles))
    return (output, log_total)


def attend_backward(
    queries,
    key_all,
    value_all,
    seg_all,
    pos_all,
    segment_ids,
    positions,
    log_total,
    output_grad,
    output,
):
    key_count = key_all.shape[0]
    key_tiles, value_tiles, seg_tiles, pos_tiles = split_tiles(key_all, value_all, seg_all, pos_all)
    row_delta = jnp.einsum("nhjd,nhjd->hjn", output_grad.astype(jnp.float32), output)

    def grad_step(query_sum, pieces):
        key_tile, value_tile, seg_key, pos_key = pieces
        allowed = tile_mask(segment_ids, positions, seg_key, pos_key)
        scores = tile_scores(queries, key_tile, allowed)
        weights_tile = jnp.where(allowed, jnp.exp(scores - log_total[..., None]), 0.0)
        value_grad = jnp.einsum(
            "hjnk,nhjd->khd",
            weights_tile.astype(jnp.bfloat16),
            output_grad,
            preferred_element_type=jnp.float32,
        )
        weight_grad = jnp.einsum(
            "nhjd,khd->hjnk", output_grad, value_tile, preferred_element_type=jnp.float32
        )
        score_grad = (weights_tile * (weight_grad - row_delta[..., None])).astype(jnp.bfloat16)
        query_sum = query_sum + jnp.einsum(
            "hjnk,khd->nhjd", score_grad, key_tile, preferred_element_type=jnp.float32
        )
        key_grad = jnp.einsum(
            "hjnk,nhjd->khd", score_grad, queries, preferred_element_type=jnp.float32
        )
        return (query_sum, (key_grad, value_grad))

    start_query = jnp.zeros(queries.shape, jnp.float32)
    query_sum, (key_grads, value_grads) = lax.scan(
        grad_step, start_query, (key_tiles, value_tiles, seg_tiles, pos_tiles)
    )
    scale_factor = HEAD_DIM ** (-0.5)
    return (
        query_sum * scale_factor,
        key_grads.reshape(key_count, KW) * scale_factor,
        value_grads.reshape(key_count, KW),
    )


def local(
    tokens,
    segment_ids,
    positions,
    attend_gain,
    query_key_value,
    attend_out,
    feed_gain,
    gate_up,
    down_weight,
    upstream,
):
    local_rows = tokens.shape[0]
    head_ratio = HEADS // KV_HEADS
    inputs = tokens.astype(jnp.float32)
    factor_one = rms_factor(inputs)
    normed_one = (inputs * factor_one * attend_gain).astype(jnp.bfloat16)
    full_qkv, full_out, full_gate_up, full_down = (
        lax.all_gather(query_key_value, "wsh", axis=0, tiled=True),
        lax.all_gather(attend_out, "wsh", axis=0, tiled=True),
        lax.all_gather(gate_up, "wsh", axis=0, tiled=True),
        lax.all_gather(down_weight, "wsh", axis=0, tiled=True),
    )
    projected = jnp.dot(normed_one, full_qkv, preferred_element_type=jnp.float32)
    cosine, sine_table = rope_angles(positions)
    queries = rotate(
        projected[:, :QW].reshape(local_rows, HEADS, HEAD_DIM), cosine, sine_table
    ).astype(jnp.bfloat16)
    queries = queries.reshape(local_rows, KV_HEADS, head_ratio, HEAD_DIM)
    key_local = (
        rotate(
            projected[:, QW : QW + KW].reshape(local_rows, KV_HEADS, HEAD_DIM), cosine, sine_table
        )
        .astype(jnp.bfloat16)
        .reshape(local_rows, KW)
    )
    value_local = projected[:, QW + KW :].astype(jnp.bfloat16)
    key_all, value_all, seg_all, pos_all = (
        lax.all_gather(key_local, ("ctx", "wsh"), axis=0, tiled=True),
        lax.all_gather(value_local, ("ctx", "wsh"), axis=0, tiled=True),
        lax.all_gather(segment_ids, ("ctx", "wsh"), axis=0, tiled=True),
        lax.all_gather(positions, ("ctx", "wsh"), axis=0, tiled=True),
    )
    output, log_total = attend_forward(
        queries, key_all, value_all, seg_all, pos_all, segment_ids, positions
    )
    attended = output.reshape(local_rows, QW).astype(jnp.bfloat16)
    middle = inputs + jnp.dot(attended, full_out, preferred_element_type=jnp.float32)
    factor_two = rms_factor(middle)
    normed_two = (middle * factor_two * feed_gain).astype(jnp.bfloat16)
    gate_value = jnp.dot(normed_two, full_gate_up, preferred_element_type=jnp.float32)
    gate_part = gate_value[:, :FF]
    up_part = gate_value[:, FF:]
    sigmoid_gate = jax.nn.sigmoid(gate_part)
    silu_gate = gate_part * sigmoid_gate
    hidden = (silu_gate * up_part).astype(jnp.bfloat16)
    activations = (middle + jnp.dot(hidden, full_down, preferred_element_type=jnp.float32)).astype(
        jnp.bfloat16
    )
    back_qkv, back_out, back_gate_up, back_down = (
        lax.all_gather(query_key_value, "wsh", axis=0, tiled=True),
        lax.all_gather(attend_out, "wsh", axis=0, tiled=True),
        lax.all_gather(gate_up, "wsh", axis=0, tiled=True),
        lax.all_gather(down_weight, "wsh", axis=0, tiled=True),
    )
    down_grad = jnp.dot(hidden.T, upstream, preferred_element_type=jnp.float32)
    hidden_grad = jnp.dot(upstream, back_down.T, preferred_element_type=jnp.float32)
    gate_grad = hidden_grad * up_part * sigmoid_gate * (1.0 + gate_part * (1.0 - sigmoid_gate))
    up_grad = hidden_grad * silu_gate
    joint_grad = jnp.concatenate([gate_grad, up_grad], axis=1).astype(jnp.bfloat16)
    gate_up_grad = jnp.dot(normed_two.T, joint_grad, preferred_element_type=jnp.float32)
    normed_two_grad = jnp.dot(joint_grad, back_gate_up.T, preferred_element_type=jnp.float32)
    middle_part, feed_gain_grad = norm_back(normed_two_grad, middle, factor_two, feed_gain)
    middle_grad = upstream.astype(jnp.float32) + middle_part
    branch_grad = middle_grad.astype(jnp.bfloat16)
    out_weight_grad = jnp.dot(attended.T, branch_grad, preferred_element_type=jnp.float32)
    attended_grad = jnp.dot(branch_grad, back_out.T, preferred_element_type=jnp.float32).astype(
        jnp.bfloat16
    )
    attended_grad = attended_grad.reshape(local_rows, KV_HEADS, head_ratio, HEAD_DIM)
    query_grad, key_grad_all, value_grad_all = attend_backward(
        queries,
        key_all,
        value_all,
        seg_all,
        pos_all,
        segment_ids,
        positions,
        log_total,
        attended_grad,
        output,
    )
    key_grad, value_grad = (
        lax.psum_scatter(key_grad_all, ("ctx", "wsh"), scatter_dimension=0, tiled=True),
        lax.psum_scatter(value_grad_all, ("ctx", "wsh"), scatter_dimension=0, tiled=True),
    )
    query_back = unrotate(
        rounded(query_grad).reshape(local_rows, HEADS, HEAD_DIM), cosine, sine_table
    ).reshape(local_rows, QW)
    key_back = unrotate(
        rounded(key_grad).reshape(local_rows, KV_HEADS, HEAD_DIM), cosine, sine_table
    ).reshape(local_rows, KW)
    projected_grad = jnp.concatenate(
        [
            query_back.astype(jnp.bfloat16),
            key_back.astype(jnp.bfloat16),
            value_grad.astype(jnp.bfloat16),
        ],
        axis=1,
    )
    qkv_grad = jnp.dot(normed_one.T, projected_grad, preferred_element_type=jnp.float32)
    normed_one_grad = jnp.dot(projected_grad, back_qkv.T, preferred_element_type=jnp.float32)
    input_part, attend_gain_grad = norm_back(normed_one_grad, inputs, factor_one, attend_gain)
    input_grad = middle_grad + input_part
    shares = (
        lax.psum_scatter(qkv_grad, ("ctx", "wsh"), scatter_dimension=0, tiled=True),
        lax.psum_scatter(out_weight_grad, ("ctx", "wsh"), scatter_dimension=0, tiled=True),
        lax.psum_scatter(gate_up_grad, ("ctx", "wsh"), scatter_dimension=0, tiled=True),
        lax.psum_scatter(down_grad, ("ctx", "wsh"), scatter_dimension=0, tiled=True),
        lax.psum_scatter(attend_gain_grad, ("ctx", "wsh"), scatter_dimension=0, tiled=True),
        lax.psum_scatter(feed_gain_grad, ("ctx", "wsh"), scatter_dimension=0, tiled=True),
    )
    shares = (
        lax.psum(shares[0].astype(jnp.bfloat16), "grp").astype(jnp.float32),
        lax.psum(shares[1].astype(jnp.bfloat16), "grp").astype(jnp.float32),
        lax.psum(shares[2].astype(jnp.bfloat16), "grp").astype(jnp.float32),
        lax.psum(shares[3].astype(jnp.bfloat16), "grp").astype(jnp.float32),
        lax.psum(shares[4].astype(jnp.bfloat16), "grp").astype(jnp.float32),
        lax.psum(shares[5].astype(jnp.bfloat16), "grp").astype(jnp.float32),
    )
    return (
        activations,
        input_grad,
        shares[0],
        shares[1],
        shares[2],
        shares[3],
        shares[4],
        shares[5],
    )


def solution(mesh):
    in_specs = (
        P(("grp", "ctx", "wsh"), None),
        P(("grp", "ctx", "wsh")),
        P(("grp", "ctx", "wsh")),
        P(),
        P("wsh", None),
        P("wsh", None),
        P(),
        P("wsh", None),
        P("wsh", None),
        P(("grp", "ctx", "wsh"), None),
    )
    out_specs = (
        P(("grp", "ctx", "wsh"), None),
        P(("grp", "ctx", "wsh"), None),
        P(("ctx", "wsh"), None),
        P(("ctx", "wsh"), None),
        P(("ctx", "wsh"), None),
        P(("ctx", "wsh"), None),
        P(("ctx", "wsh")),
        P(("ctx", "wsh")),
    )
    return jax.shard_map(local, mesh=mesh, in_specs=in_specs, out_specs=out_specs, check_vma=False)
```

profile of v0, /device:TPU:0, one launch (start us, length us, event | category | flops | bytes accessed | tf_op | source)
XLA Modules:
  0.0 1910.9 jit_solution(1182851010017177751)
XLA Ops:
  10.6 56.6 %all-gather.7.cloned.1.call-done = bf16[1152,1920]{1,0:T(8,128)(2,1)} async-done(((bf16[288,1920]{1,0:T(8,128)(2,1)}), bf16[1152,1920]{1,0:T(8,128)(2,1)}) %all-gather.7.cloned.1.call-update) | async-done | bytes 4423696 | tf_op jit(solution)/shard_map/all_gather | solution.py:205
  67.2 3.7 fusion.69
  77.2 76.4 %all-reduce.6 = (s32[3072]{0:T(1024)S(1)}, s32[3072]{0:T(1024)S(1)}) all-reduce(s32[3072]{0:T(1024)S(1)} %dynamic-update-slice, s32[3072]{0:T(1024)S(1)} %dynamic-update-slice.1), channel_id=1, replica_groups=mesh['grp'=2,'ctx'=4,'wsh'=4] {'ctx','wsh'}, use_global_device_ids=true, to_apply=%add | all-reduce | flops 6144 | bytes 49152
  154.3 8.1 reshape.216
  162.4 6.0 copy.46
  168.4 31.3 %all-gather.9.cloned.1.call-done = bf16[3072,384]{1,0:T(8,128)(2,1)} async-done(((bf16[192,384]{1,0:T(8,128)(2,1)}), bf16[3072,384]{1,0:T(8,128)(2,1)}) %all-gather.9.cloned.1.call-update) | async-done | bytes 2359312 | tf_op jit(solution)/shard_map/all_gather | solution.py:226
  199.7 8.1 reshape.215
  207.8 7.2 copy.45
  215.0 24.5 %while.39 = (s32[]{:T(128)}, f32[6,3,192]{2,1,0:T(4,128)S(1)}, f32[6,3,192]{2,1,0:T(4,128)S(1)}, s32[3,1024]{1,0:T(4,128)S(1)}, s32[192]{0:T(256)S(1)}, /*index=...) while((s32[]{:T(128)}, f32[6,3,192]{2,1,0:T(4,128)S(1)}, ...), condition=%wide.region_4.5_spmd.clone, body=%wide.region_1.4_spmd.clone.sunk | while | flops 482101120 | bytes 30485644 | solution.py:111
  218.6 4.6 select_reduce_fusion.2
  226.8 4.5 select_reduce_fusion.2
  235.0 4.6 select_reduce_fusion.2
  240.2 29.6 %while.40 = (s32[]{:T(128)}, f32[192,6,3,64]{0,3,2,1:T(8,128)}, bf16[3,1024,6,64]{1,3,2,0:T(8,128)(2,1)}, s32[3,1024]{1,0:T(4,128)S(1)}, s32[192]{0:T(256)S(1)},...) while((s32[]{:T(128)}, f32[192,6,3,64]{0,3,2,1:T(8,128)}, ...), condition=%wide.region_6.7_spmd.clone, body=%wide.region_5.6_spmd.clone.sunk | while | flops 924894208 | bytes 4674702 | solution.py:132
  242.0 7.8 fusion.126
  251.5 8.5 fusion.126
  261.7 8.2 fusion.126
  272.0 3.7 multiply_reduce_fusion.2
  275.7 101.8 %all-gather.15.cloned.1.call-done = bf16[1152,6144]{1,0:T(8,128)(2,1)} async-done(((bf16[288,6144]{1,0:T(8,128)(2,1)}), bf16[1152,6144]{1,0:T(8,128)(2,1)}) %all-gather.15.cloned.1.call-update) | async-done | bytes 14155792 | tf_op jit(solution)/shard_map/all_gather | solution.py:207
  377.5 11.0 fusion.75
  388.5 67.5 %all-gather.17.cloned.1.call-done = bf16[3072,1152]{1,0:T(8,128)(2,1)} async-done(((bf16[768,1152]{1,0:T(8,128)(2,1)}), bf16[3072,1152]{1,0:T(8,128)(2,1)}) %all-gather.17.cloned.1.call-update) | async-done | bytes 7077904 | tf_op jit(solution)/shard_map/all_gather | solution.py:208
  455.9 8.8 multiply_convert_fusion.1
  464.7 11.3 multiply_reduce_fusion
  483.2 67.5 %while.41 = (s32[]{:T(128)}, f32[192,6,3,64]{0,3,2,1:T(8,128)}, f32[3,1024,6,64]{1,3,2,0:T(8,128)}, f32[3,1024,6,64]{1,3,2,0:T(8,128)}, bf16[3,1024,6,64]{1,3,2,...) while((s32[]{:T(128)}, f32[192,6,3,64]{0,3,2,1:T(8,128)}, ...), condition=%wide.region_10.11_spmd.clone, body=%wide.region_9.10_spmd.clone.sunk | while | flops 2308621312 | bytes 81001752 | solution.py:176
  487.4 6.0 bitcast_dynamic-update-slice_fusion.5
  493.4 7.3 fusion.138
  509.7 6.1 bitcast_dynamic-update-slice_fusion.5
  515.8 7.3 fusion.138
  532.1 6.0 bitcast_dynamic-update-slice_fusion.5
  538.1 7.4 fusion.138
  548.0 2.7 bitcast_dynamic-update-slice_fusion.4
  550.8 5.5 broadcast_multiply_fusion
  556.3 9.2 copy.76
  565.5 10.3 reshape.207
  575.9 9.2 copy.77
  585.1 10.4 reshape.209
  596.9 3.3 fusion.65
  602.1 111.3 %reduce-scatter.19.cloned.1.call-done = f32[192,384]{1,0:T(8,128)} async-done(((f32[3072,384]{1,0:T(8,128)}), f32[192,384]{1,0:T(8,128)}) %reduce-scatter.19.cloned.1.call-update) | async-done | bytes 294928
  714.5 141.3 %reduce-scatter.21.cloned.1.call-done = f32[192,384]{1,0:T(8,128)} async-done(((f32[3072,384]{1,0:T(8,128)}), f32[192,384]{1,0:T(8,128)}) %reduce-scatter.21.cloned.1.call-update) | async-done | bytes 294928
  857.0 5.0 fusion.63
  863.0 8.6 fusion.77
  872.8 12.6 fusion.51
  886.2 115.2 %reduce-scatter.25.cloned.1.call-done = f32[72,1152]{1,0:T(8,128)} async-done(((f32[1152,1152]{1,0:T(8,128)}), f32[72,1152]{1,0:T(8,128)}) %reduce-scatter.25.cloned.1.call-update) | async-done | bytes 331792
  1003.0 170.2 %reduce-scatter.23.cloned.1.call-done = f32[72,1920]{1,0:T(8,128)} async-done(((f32[1152,1920]{1,0:T(8,128)}), f32[72,1920]{1,0:T(8,128)}) %reduce-scatter.23.cloned.1.call-update) | async-done | bytes 552976
  1175.0 224.2 %reduce-scatter.17.cloned.1.call-done = f32[192,1152]{1,0:T(8,128)} async-done(((f32[3072,1152]{1,0:T(8,128)}), f32[192,1152]{1,0:T(8,128)}) %reduce-scatter.17.cloned.1.call-update) | async-done | bytes 884752 | tf_op jit(solution)/shard_map/reduce_scatter | solution.py:305
  1401.1 403.0 %reduce-scatter.15.cloned.1.call-done = f32[72,6144]{1,0:T(8,128)} async-done(((f32[1152,6144]{1,0:T(8,128)}), f32[72,6144]{1,0:T(8,128)}) %reduce-scatter.15.cloned.1.call-update) | async-done | bytes 1769488 | tf_op jit(solution)/shard_map/reduce_scatter | solution.py:304
  1806.6 5.9 fusion.49
  1812.5 4.1 fusion.62
  1816.6 74.8 %all-reduce.7 = (bf16[1152]{0:T(1024)(128)(2,1)S(1)}, bf16[1152]{0:T(1024)(128)(2,1)S(1)}) all-reduce(f32[1152]{0:T(1024)S(1)} %get-tuple-element.388, f32[1152]{0:T(1024)S(1)} %copy-done.29), channel_id=8, replica_groups=mesh['grp'=2,'ctx'=4,'wsh'=4] {'ctx','wsh'}, use_global_device_ids=true, to_apply=%region_23.24.clone | all-reduce | flops 2304 | bytes 13824
  (212 shorter events, 87.9 us)
Async XLA Ops:
  7.2 60.0 %all-gather.7.cloned.1.call-start = ((), (), s32[]{:S(2)}) async-start(), calls=%async_computation.6 | async-start | bytes 5529600 | tf_op jit(solution)/shard_map/all_gather | solution.py:205
  7.9 146.4 %all-gather.11.cloned.1.call-start = ((), (), s32[]{:S(2)}) async-start(), calls=%async_computation.8 | async-start | bytes 2506752 | tf_op jit(solution)/shard_map/all_gather | solution.py:225
  10.4 60.5 %copy-start.26 = (f32[192]{0:T(256)}, f32[192]{0:T(256)S(1)}, u32[]{:S(2)}) copy-start(f32[192]{0:T(256)S(1)} %get-tuple-element.488) | copy-start | bytes 2308
  10.6 143.4 %copy-start.14 = (f32[192,32]{0,1:T(8,128)}, f32[192,32]{0,1:T(8,128)S(1)}, u32[]{:S(2)}) copy-start(f32[192,32]{0,1:T(8,128)S(1)} %get-tuple-element.485) | copy-start | bytes 73732
  10.6 143.4 %copy-start.16 = (f32[192,32]{0,1:T(8,128)}, f32[192,32]{0,1:T(8,128)S(1)}, u32[]{:S(2)}) copy-start(f32[192,32]{0,1:T(8,128)S(1)} %get-tuple-element.486) | copy-start | bytes 73732
  71.2 3.5 copy-start.31
  71.2 4.8 copy-start.19
  72.0 127.7 %all-gather.9.cloned.1.call-start = ((), (), s32[]{:S(2)}) async-start(), calls=%async_computation.7 | async-start | bytes 2506752 | tf_op jit(solution)/shard_map/all_gather | solution.py:226
  72.8 199.3 %all-gather.13.cloned.1.call-start = ((), (), s32[]{:S(2)}) async-start(), calls=%async_computation.9 | async-start | bytes 3317760 | tf_op jit(solution)/shard_map/all_gather | solution.py:206
  73.3 304.2 %all-gather.15.cloned.1.call-start = ((), (), s32[]{:S(2)}) async-start(), calls=%async_computation.10 | async-start | bytes 17694720 | tf_op jit(solution)/shard_map/all_gather | solution.py:207
  73.9 382.0 %all-gather.17.cloned.1.call-start = ((), (), s32[]{:S(2)}) async-start(), calls=%async_computation.11 | async-start | bytes 8847360 | tf_op jit(solution)/shard_map/all_gather | solution.py:208
  74.5 638.9 %reduce-scatter.19.cloned.1.call-start = ((), (), s32[]{:S(2)}) async-start(), calls=%async_computation.14 | async-start | bytes 5013504
  240.2 31.8 %copy-start.7 = (bf16[192,1152]{1,0:T(8,128)(2,1)S(1)}, bf16[192,1152]{1,0:T(8,128)(2,1)}, u32[]{:S(2)}) copy-start(bf16[192,1152]{1,0:T(8,128)(2,1)} %param.16) | copy-start | bytes 1327108
  269.8 118.6 %copy-start.18 = (s32[3,1024]{1,0:T(4,128)}, s32[3,1024]{1,0:T(4,128)S(1)}, u32[]{:S(2)}) copy-start(s32[3,1024]{1,0:T(4,128)S(1)} %get-tuple-element.899) | copy-start | bytes 36868
  269.8 118.6 %copy-start.20 = (s32[192]{0:T(256)}, s32[192]{0:T(256)S(1)}, u32[]{:S(2)}) copy-start(s32[192]{0:T(256)S(1)} %get-tuple-element.902) | copy-start | bytes 2308
  269.8 107.7 %copy-start.21 = (f32[1152]{0:T(1024)S(1)}, f32[1152]{0:T(1024)}, u32[]{:S(2)}) copy-start(f32[1152]{0:T(1024)} %param.22) | copy-start | bytes 13828
  275.7 200.3 %copy-start.24 = (f32[192]{0:T(256)}, f32[192]{0:T(256)S(1)}, u32[]{:S(2)}) copy-start(f32[192]{0:T(256)S(1)} %get-tuple-element.490) | copy-start | bytes 2308
  377.5 78.4 %copy-start.11 = (bf16[192,1152]{1,0:T(8,128)(2,1)S(1)}, bf16[192,1152]{1,0:T(8,128)(2,1)}, u32[]{:S(2)}) copy-start(bf16[192,1152]{1,0:T(8,128)(2,1)} %param.25) | copy-start | bytes 1327108
  455.9 8.8 copy-start.3
  464.7 11.3 copy-start.13
  476.0 2.1 copy-start.9
  487.4 6.1 copy-start.28
  493.4 7.4 copy-start
  503.3 2.7 copy-start.1
  509.7 6.1 copy-start.28
  515.8 7.4 copy-start
  525.7 2.6 copy-start.1
  532.1 6.1 copy-start.28
  538.1 7.4 copy-start
  548.0 2.7 copy-start.1
  575.9 279.9 %reduce-scatter.21.cloned.1.call-start = ((), (), s32[]{:S(2)}) async-start(), calls=%async_computation.15 | async-start | bytes 5013504
  595.5 1.2 copy-start.6
  595.5 1.4 copy-start.10
  595.6 405.8 %reduce-scatter.25.cloned.1.call-start = ((), (), s32[]{:S(2)}) async-start(), calls=%async_computation.17 | async-start | bytes 5640192
  600.2 1.3 copy-start.2
  600.2 1.6 copy-start.15
  600.2 1.6 copy-start.17
  600.2 573.0 %reduce-scatter.23.cloned.1.call-start = ((), (), s32[]{:S(2)}) async-start(), calls=%async_computation.16 | async-start | bytes 9400320
  601.6 255.4 %copy-start.8 = (bf16[192,1152]{1,0:T(8,128)(2,1)S(1)}, bf16[192,1152]{1,0:T(8,128)(2,1)}, u32[]{:S(2)}) copy-start(bf16[192,1152]{1,0:T(8,128)(2,1)} %param.16) | copy-start | bytes 1327108
  601.6 255.4 %copy-start.23 = (f32[1152]{0:T(1024)S(1)}, f32[1152]{0:T(1024)}, u32[]{:S(2)}) copy-start(f32[1152]{0:T(1024)} %param.19) | copy-start | bytes 13828
  601.6 255.4 %copy-start.27 = (f32[192]{0:T(256)S(1)}, f32[192]{0:T(256)}, u32[]{:S(2)}) copy-start(f32[192]{0:T(256)} %copy-done.26) | copy-start | bytes 2308
  862.1 537.1 %reduce-scatter.17.cloned.1.call-start = ((), (), s32[]{:S(2)}) async-start(), calls=%async_computation.13 | async-start | bytes 15040512 | tf_op jit(solution)/shard_map/reduce_scatter | solution.py:305
  871.6 1.2 copy-start.22
  871.6 1.2 copy-start.25
  871.7 932.5 %reduce-scatter.15.cloned.1.call-start = ((), (), s32[]{:S(2)}) async-start(), calls=%async_computation.12 | async-start | bytes 30081024 | tf_op jit(solution)/shard_map/reduce_scatter | solution.py:304
  885.4 1010.8 %all-reduce.12.cloned.1.call-start = ((), (), s32[]{:S(2)}) async-start(), calls=%async_computation.18 | async-start | bytes 3538944 | tf_op jit(solution)/shard_map/psum | solution.py:310
  1812.5 4.1 copy-start.29
  1812.5 82.5 %copy-start.30 = (f32[192]{0:T(256)S(1)}, f32[192]{0:T(256)}, u32[]{:S(2)}) copy-start(f32[192]{0:T(256)} %get-tuple-element.487) | copy-start | bytes 2308
  (3 other events, 3.1 us)
Sparse Core Ops, SparseCore 0:
  9.8 57.3 all-gather.6
  72.1 62.8 all-gather.10
  138.4 61.2 all-gather.8
  201.4 38.7 all-gather.12
  241.9 135.5 all-gather.14
  379.2 76.6 all-gather.16
  576.0 137.3 reduce-scatter.18
  719.4 136.3 reduce-scatter.20
  861.1 140.2 reduce-scatter.24
  1006.9 166.2 reduce-scatter.22
  1179.0 220.1 reduce-scatter.16
  1405.8 398.3 reduce-scatter.14
  1807.4 19.9 all-reduce.11
where the time goes:
time: 1920 us; the launch traced here: 1910 us
  waiting for transfers between devices  1420 us (74%)
  matrix products  173 us (9%)
  blocking collectives  154 us (8%)
  local copies, waits for them, and re-layouts  82.4 us (4%)
  other arithmetic  59.4 us (3%)
    unnamed x17, waiting for transfers between devices  540 us
    reduce_scatter x1, waiting for transfers between devices, local(): lax.psum_scatter(gate_up_grad, ('ctx', 'wsh'), scatter_dimension=0, tiled...  403 us
    reduce_scatter x1, waiting for transfers between devices, local(): lax.psum_scatter(down_grad, ('ctx', 'wsh'), scatter_dimension=0, tiled=True)  224 us
    unnamed x2, blocking collectives  151 us
    all_gather x1, waiting for transfers between devices, local(): lax.all_gather(gate_up, 'wsh', axis=0, tiled=True)  102 us
    all_gather x1, waiting for transfers between devices, local(): lax.all_gather(down_weight, 'wsh', axis=0, tiled=True)  67.5 us
    unnamed x73, local copies, waits for them, and re-layouts  62.7 us
    all_gather x1, waiting for transfers between devices, local(): lax.all_gather(query_key_value, 'wsh', axis=0, tiled=True)  56.6 us
  transfers between devices with their start and end apart: 13, of which 10 were waited for; matrix products, arithmetic and copies ran while one was open for 9% of the time, Pallas kernels for 0%

commit v1 on v0

--- a/solution.py
+++ b/solution.py
@@ -12,6 +12,22 @@
 QW = 1152
 KW = 384
 EPSILON = 1e-05
+
+
+def gather_around(x, axis, dim):
+    ways, here, hop = (lax.axis_size(axis), lax.axis_index(axis), x.shape[dim])
+    shape = [n * ways if d == dim else n for d, n in enumerate(x.shape)]
+    full = lax.dynamic_update_slice_in_dim(jnp.zeros(shape, x.dtype), x, here * hop, axis=dim)
+    going_up = going_down = x
+    for far in range(1, ways // 2 + 1):
+        going_up = lax.ppermute(going_up, axis, [(d, (d + 1) % ways) for d in range(ways)])
+        full = lax.dynamic_update_slice_in_dim(full, going_up, (here - far) % ways * hop, axis=dim)
+        if 2 * far < ways:
+            going_down = lax.ppermute(going_down, axis, [(d, (d - 1) % ways) for d in range(ways)])
+            full = lax.dynamic_update_slice_in_dim(
+                full, going_down, (here + far) % ways * hop, axis=dim
+            )
+    return full
 
 
 def rope_angles(positions):
@@ -205,7 +221,7 @@
         lax.all_gather(query_key_value, "wsh", axis=0, tiled=True),
         lax.all_gather(attend_out, "wsh", axis=0, tiled=True),
         lax.all_gather(gate_up, "wsh", axis=0, tiled=True),
-        lax.all_gather(down_weight, "wsh", axis=0, tiled=True),
+        gather_around(down_weight, "wsh", 0),
     )
     projected = jnp.dot(normed_one, full_qkv, preferred_element_type=jnp.float32)
     cosine, sine_table = rope_angles(positions)

time: 1920 us -> 2000 us (1.042)
  matrix products: 173 us -> 214 us
  local copies, waits for them, and re-layouts: 82.4 us -> 103 us
  waiting for transfers between devices: 1420 us -> 1440 us
    ppermute x0 -> x3, waiting for transfers between devices: none -> 120 us  [the longest x2 86.3 us: gather_around(): lax.ppermute(going_up, axis, [(d, (d + 1) % ways) for d in range(ways)])]
    unnamed x17, waiting for transfers between devices: 540 us -> 456 us
  transfers between devices with their start and end apart: 13 -> 16, of which waited for: 10 -> 13; matrix products, arithmetic and copies ran while one was open for 9% -> 10% of each run, Pallas kernels for 0% -> 0%
where the time goes in v1:
time: 2000 us; the launch traced here: 1990 us
  waiting for transfers between devices  1440 us (72%)
  matrix products  214 us (11%)
  blocking collectives  154 us (8%)
  local copies, waits for them, and re-layouts  103 us (5%)
  other arithmetic  59.4 us (3%)
    unnamed x17, waiting for transfers between devices  456 us
    reduce_scatter x1, waiting for transfers between devices, local(): lax.psum_scatter(gate_up_grad, ('ctx', 'wsh'), scatter_dimension=0, tiled...  403 us
    reduce_scatter x1, waiting for transfers between devices, local(): lax.psum_scatter(down_grad, ('ctx', 'wsh'), scatter_dimension=0, tiled=True)  224 us
    unnamed x2, blocking collectives  151 us
    ppermute x2, waiting for transfers between devices, gather_around(): lax.ppermute(going_up, axis, [(d, (d + 1) % ways) for d in range(ways)])  86.3 us
    all_gather x1, waiting for transfers between devices, local(): lax.all_gather(gate_up, 'wsh', axis=0, tiled=True)  83.2 us
    all_gather x1, waiting for transfers between devices, local(): lax.all_gather(down_weight, 'wsh', axis=0, tiled=True)  67.5 us
    unnamed x73, local copies, waits for them, and re-layouts  61.7 us
  transfers between devices with their start and end apart: 16, of which 13 were waited for; matrix products, arithmetic and copies ran while one was open for 10% of the time, Pallas kernels for 0%

profile of v1, /device:TPU:0, one launch (start us, length us, event | category | flops | bytes accessed | tf_op | source)
XLA Modules:
  0.0 1992.7 jit_solution(2669508710071281563)
XLA Ops:
  10.6 56.6 %all-gather.7.cloned.1.call-done = bf16[1152,1920]{1,0:T(8,128)(2,1)} async-done(((bf16[288,1920]{1,0:T(8,128)(2,1)}), bf16[1152,1920]{1,0:T(8,128)(2,1)}) %all-gather.7.cloned.1.call-update) | async-done | bytes 4423696 | tf_op jit(solution)/shard_map/all_gather | solution.py:221
  76.5 76.5 %all-reduce.6 = (s32[3072]{0:T(1024)S(1)}, s32[3072]{0:T(1024)S(1)}) all-reduce(s32[3072]{0:T(1024)S(1)} %dynamic-update-slice, s32[3072]{0:T(1024)S(1)} %dynamic-update-slice.1), channel_id=1, replica_groups=mesh['grp'=2,'ctx'=4,'wsh'=4] {'ctx','wsh'}, use_global_device_ids=true, to_apply=%add | all-reduce | flops 6144 | bytes 49152
  153.9 8.1 reshape.216
  168.1 31.7 %all-gather.9.cloned.1.call-done = bf16[3072,384]{1,0:T(8,128)(2,1)} async-done(((bf16[192,384]{1,0:T(8,128)(2,1)}), bf16[3072,384]{1,0:T(8,128)(2,1)}) %all-gather.9.cloned.1.call-update) | async-done | bytes 2359312 | tf_op jit(solution)/shard_map/all_gather | solution.py:242
  199.8 8.1 reshape.215
  207.9 7.2 copy.45
  215.1 46.0 %while.39 = (s32[]{:T(128)}, f32[6,3,192]{2,1,0:T(4,128)S(1)}, f32[6,3,192]{2,1,0:T(4,128)S(1)}, s32[3,1024]{1,0:T(4,128)S(1)}, s32[192]{0:T(256)S(1)}, /*index=...) while((s32[]{:T(128)}, f32[6,3,192]{2,1,0:T(4,128)S(1)}, ...), condition=%wide.region_4.5_spmd.clone, body=%wide.region_1.4_spmd.clone.sunk | while | flops 482101120 | bytes 30485636 | solution.py:127
  215.4 6.4 fusion.121
  221.8 8.0 select_reduce_fusion.2
  230.3 6.4 fusion.121
  236.7 7.6 select_reduce_fusion.2
  244.7 8.0 fusion.121
  252.7 8.4 select_reduce_fusion.2
  261.2 27.3 %while.40 = (s32[]{:T(128)}, f32[192,6,3,64]{0,3,2,1:T(8,128)}, bf16[3,1024,6,64]{1,3,2,0:T(8,128)(2,1)}, s32[3,1024]{1,0:T(4,128)S(1)}, s32[192]{0:T(256)S(1)},...) while((s32[]{:T(128)}, f32[192,6,3,64]{0,3,2,1:T(8,128)}, ...), condition=%wide.region_6.7_spmd.clone, body=%wide.region_5.6_spmd.clone.sunk | while | flops 924894208 | bytes 4674183 | solution.py:148
  262.2 7.7 fusion.126
  271.0 8.2 fusion.126
  280.1 8.2 fusion.126
  294.4 83.2 %all-gather.15.cloned.1.call-done = bf16[1152,6144]{1,0:T(8,128)(2,1)} async-done(((bf16[288,6144]{1,0:T(8,128)(2,1)}), bf16[1152,6144]{1,0:T(8,128)(2,1)}) %all-gather.15.cloned.1.call-update) | async-done | bytes 14155792 | tf_op jit(solution)/shard_map/all_gather | solution.py:223
  377.6 11.0 fusion.75
  388.5 67.5 %all-gather.17.cloned.1.call-done = bf16[3072,1152]{1,0:T(8,128)(2,1)} async-done(((bf16[768,1152]{1,0:T(8,128)(2,1)}), bf16[3072,1152]{1,0:T(8,128)(2,1)}) %all-gather.17.cloned.1.call-update) | async-done | bytes 7077904 | tf_op jit(solution)/shard_map/all_gather | solution.py:266
  456.0 8.8 multiply_convert_fusion.1
  464.8 11.3 multiply_reduce_fusion
  482.9 98.4 %while.41 = (s32[]{:T(128)}, f32[192,6,3,64]{0,3,2,1:T(8,128)}, f32[3,1024,6,64]{1,3,2,0:T(8,128)}, f32[3,1024,6,64]{1,3,2,0:T(8,128)}, bf16[3,1024,6,64]{1,3,2,...) while((s32[]{:T(128)}, f32[192,6,3,64]{0,3,2,1:T(8,128)}, ...), condition=%wide.region_10.11_spmd.clone, body=%wide.region_9.10_spmd.clone.sunk | while | flops 2308621312 | bytes 158783216 | solution.py:192
  485.7 8.0 fusion.138
  499.2 6.4 fusion.139
  505.6 10.2 bitcast_dynamic-update-slice_fusion.5
  518.2 8.0 fusion.138
  531.7 6.7 fusion.139
  538.4 10.2 bitcast_dynamic-update-slice_fusion.5
  550.9 8.0 fusion.138
  564.5 6.7 fusion.139
  571.2 10.1 bitcast_dynamic-update-slice_fusion.5
  586.7 9.2 copy.76
  595.9 10.4 reshape.207
  606.4 9.4 copy.77
  615.7 10.4 reshape.209
  632.7 111.2 %reduce-scatter.19.cloned.1.call-done = f32[192,384]{1,0:T(8,128)} async-done(((f32[3072,384]{1,0:T(8,128)}), f32[192,384]{1,0:T(8,128)}) %reduce-scatter.19.cloned.1.call-update) | async-done | bytes 294928
  745.1 141.3 %reduce-scatter.21.cloned.1.call-done = f32[192,384]{1,0:T(8,128)} async-done(((f32[3072,384]{1,0:T(8,128)}), f32[192,384]{1,0:T(8,128)}) %reduce-scatter.21.cloned.1.call-update) | async-done | bytes 294928
  893.7 8.5 fusion.77
  903.4 12.6 fusion.51
  919.1 49.5 %collective-permute-done = bf16[768,1152]{1,0:T(8,128)(2,1)} collective-permute-done((bf16[768,1152]{1,0:T(8,128)(2,1)}, bf16[768,1152]{1,0:T(8,128)(2,1)}, u32[]{:S(2)}, u32[]{:S(2)}) %collective-permute-start) | collective-permute-done | bytes 1769504 | tf_op jit(solution)/shard_map/ppermute | solution.py:23
  976.9 34.0 %collective-permute-done.1 = bf16[768,1152]{1,0:T(8,128)(2,1)} collective-permute-done((bf16[768,1152]{1,0:T(8,128)(2,1)}, bf16[768,1152]{1,0:T(8,128)(2,1)}, u32[]{:S(2)}, u32[]{:S(2)}) %collective-permute-start.1) | collective-permute-done | bytes 1769504 | tf_op jit(solution)/shard_map/ppermute | solution.py:26
  1013.9 36.8 %collective-permute-done.2 = bf16[768,1152]{1,0:T(8,128)(2,1)} collective-permute-done((bf16[768,1152]{1,0:T(8,128)(2,1)}, bf16[768,1152]{1,0:T(8,128)(2,1)}, u32[]{:S(2)}, u32[]{:S(2)}) %collective-permute-start.2) | collective-permute-done | bytes 1769504 | tf_op jit(solution)/shard_map/ppermute | solution.py:23
  1053.5 31.0 %reduce-scatter.25.cloned.1.call-done = f32[72,1152]{1,0:T(8,128)} async-done(((f32[1152,1152]{1,0:T(8,128)}), f32[72,1152]{1,0:T(8,128)}) %reduce-scatter.25.cloned.1.call-update) | async-done | bytes 331792
  1086.2 170.0 %reduce-scatter.23.cloned.1.call-done = f32[72,1920]{1,0:T(8,128)} async-done(((f32[1152,1920]{1,0:T(8,128)}), f32[72,1920]{1,0:T(8,128)}) %reduce-scatter.23.cloned.1.call-update) | async-done | bytes 552976
  1258.0 224.2 %reduce-scatter.17.cloned.1.call-done = f32[192,1152]{1,0:T(8,128)} async-done(((f32[3072,1152]{1,0:T(8,128)}), f32[192,1152]{1,0:T(8,128)}) %reduce-scatter.17.cloned.1.call-update) | async-done | bytes 884752 | tf_op jit(solution)/shard_map/reduce_scatter | solution.py:321
  1484.2 402.6 %reduce-scatter.15.cloned.1.call-done = f32[72,6144]{1,0:T(8,128)} async-done(((f32[1152,6144]{1,0:T(8,128)}), f32[72,6144]{1,0:T(8,128)}) %reduce-scatter.15.cloned.1.call-update) | async-done | bytes 1769488 | tf_op jit(solution)/shard_map/reduce_scatter | solution.py:320
  1899.3 74.8 %all-reduce.7 = (bf16[1152]{0:T(1024)(128)(2,1)S(1)}, bf16[1152]{0:T(1024)(128)(2,1)S(1)}) all-reduce(f32[1152]{0:T(1024)S(1)} %get-tuple-element.388, f32[1152]{0:T(1024)S(1)} %copy-done.28), channel_id=8, replica_groups=mesh['grp'=2,'ctx'=4,'wsh'=4] {'ctx','wsh'}, use_global_device_ids=true, to_apply=%region_23.24.clone | all-reduce | flops 2304 | bytes 13824
  (217 shorter events, 126.7 us)
Async XLA Ops:
  7.2 60.0 %all-gather.7.cloned.1.call-start = ((), (), s32[]{:S(2)}) async-start(), calls=%async_computation.6 | async-start | bytes 5529600 | tf_op jit(solution)/shard_map/all_gather | solution.py:221
  7.9 145.9 %all-gather.11.cloned.1.call-start = ((), (), s32[]{:S(2)}) async-start(), calls=%async_computation.8 | async-start | bytes 2506752 | tf_op jit(solution)/shard_map/all_gather | solution.py:241
  10.4 60.5 %copy-start.26 = (f32[192]{0:T(256)}, f32[192]{0:T(256)S(1)}, u32[]{:S(2)}) copy-start(f32[192]{0:T(256)S(1)} %get-tuple-element.488) | copy-start | bytes 2308
  10.6 142.9 %copy-start.14 = (f32[192,32]{0,1:T(8,128)}, f32[192,32]{0,1:T(8,128)S(1)}, u32[]{:S(2)}) copy-start(f32[192,32]{0,1:T(8,128)S(1)} %get-tuple-element.485) | copy-start | bytes 73732
  10.6 142.9 %copy-start.16 = (f32[192,32]{0,1:T(8,128)}, f32[192,32]{0,1:T(8,128)S(1)}, u32[]{:S(2)}) copy-start(f32[192,32]{0,1:T(8,128)S(1)} %get-tuple-element.486) | copy-start | bytes 73732
  70.9 3.7 copy-start.30
  70.9 5.1 copy-start.18
  70.9 5.3 copy-start.21
  72.0 127.8 %all-gather.9.cloned.1.call-start = ((), (), s32[]{:S(2)}) async-start(), calls=%async_computation.7 | async-start | bytes 2506752 | tf_op jit(solution)/shard_map/all_gather | solution.py:242
  72.8 217.9 %all-gather.13.cloned.1.call-start = ((), (), s32[]{:S(2)}) async-start(), calls=%async_computation.9 | async-start | bytes 3317760 | tf_op jit(solution)/shard_map/all_gather | solution.py:222
  73.4 304.2 %all-gather.15.cloned.1.call-start = ((), (), s32[]{:S(2)}) async-start(), calls=%async_computation.10 | async-start | bytes 17694720 | tf_op jit(solution)/shard_map/all_gather | solution.py:223
  73.9 382.1 %all-gather.17.cloned.1.call-start = ((), (), s32[]{:S(2)}) async-start(), calls=%async_computation.11 | async-start | bytes 8847360 | tf_op jit(solution)/shard_map/all_gather | solution.py:266
  74.5 669.4 %reduce-scatter.19.cloned.1.call-start = ((), (), s32[]{:S(2)}) async-start(), calls=%async_computation.14 | async-start | bytes 5013504
  261.2 29.5 %copy-start.7 = (bf16[192,1152]{1,0:T(8,128)(2,1)S(1)}, bf16[192,1152]{1,0:T(8,128)(2,1)}, u32[]{:S(2)}) copy-start(bf16[192,1152]{1,0:T(8,128)(2,1)} %param.16) | copy-start | bytes 1327108
  288.5 89.1 %copy-start.19 = (f32[1152]{0:T(1024)S(1)}, f32[1152]{0:T(1024)}, u32[]{:S(2)}) copy-start(f32[1152]{0:T(1024)} %param.22) | copy-start | bytes 13828
  294.4 181.7 %copy-start.24 = (f32[192]{0:T(256)}, f32[192]{0:T(256)S(1)}, u32[]{:S(2)}) copy-start(f32[192]{0:T(256)S(1)} %get-tuple-element.490) | copy-start | bytes 2308
  377.6 78.4 %copy-start.11 = (bf16[192,1152]{1,0:T(8,128)(2,1)S(1)}, bf16[192,1152]{1,0:T(8,128)(2,1)}, u32[]{:S(2)}) copy-start(bf16[192,1152]{1,0:T(8,128)(2,1)} %param.25) | copy-start | bytes 1327108
  456.0 8.8 copy-start.3
  464.8 11.3 copy-start.13
  485.7 8.1 copy-start
  493.7 2.8 copy-start.1
  518.2 8.1 copy-start
  526.2 2.8 copy-start.1
  550.9 8.1 copy-start
  559.0 2.8 copy-start.1
  606.3 280.1 %reduce-scatter.21.cloned.1.call-start = ((), (), s32[]{:S(2)}) async-start(), calls=%async_computation.15 | async-start | bytes 5013504
  626.1 1.2 copy-start.6
  626.1 1.3 copy-start.9
  626.2 458.4 %reduce-scatter.25.cloned.1.call-start = ((), (), s32[]{:S(2)}) async-start(), calls=%async_computation.17 | async-start | bytes 5640192
  630.8 1.3 copy-start.2
  630.8 1.6 copy-start.15
  630.8 1.6 copy-start.17
  630.9 625.3 %reduce-scatter.23.cloned.1.call-start = ((), (), s32[]{:S(2)}) async-start(), calls=%async_computation.16 | async-start | bytes 9400320
  632.1 255.5 %copy-start.8 = (bf16[192,1152]{1,0:T(8,128)(2,1)S(1)}, bf16[192,1152]{1,0:T(8,128)(2,1)}, u32[]{:S(2)}) copy-start(bf16[192,1152]{1,0:T(8,128)(2,1)} %param.16) | copy-start | bytes 1327108
  632.1 255.5 %copy-start.22 = (f32[1152]{0:T(1024)S(1)}, f32[1152]{0:T(1024)}, u32[]{:S(2)}) copy-start(f32[1152]{0:T(1024)} %param.19) | copy-start | bytes 13828
  632.1 255.5 %copy-start.27 = (f32[192]{0:T(256)S(1)}, f32[192]{0:T(256)}, u32[]{:S(2)}) copy-start(f32[192]{0:T(256)} %copy-done.26) | copy-start | bytes 2308
  892.7 589.5 %reduce-scatter.17.cloned.1.call-start = ((), (), s32[]{:S(2)}) async-start(), calls=%async_computation.13 | async-start | bytes 15040512 | tf_op jit(solution)/shard_map/reduce_scatter | solution.py:321
  902.2 1.2 copy-start.20
  902.2 1.2 copy-start.25
  902.2 984.6 %reduce-scatter.15.cloned.1.call-start = ((), (), s32[]{:S(2)}) async-start(), calls=%async_computation.12 | async-start | bytes 30081024 | tf_op jit(solution)/shard_map/reduce_scatter | solution.py:320
  916.0 1062.9 %all-reduce.12.cloned.1.call-start = ((), (), s32[]{:S(2)}) async-start(), calls=%async_computation.18 | async-start | bytes 3538944 | tf_op jit(solution)/shard_map/psum | solution.py:326
  916.1 52.4 %collective-permute-start = (bf16[768,1152]{1,0:T(8,128)(2,1)}, bf16[768,1152]{1,0:T(8,128)(2,1)}, u32[]{:S(2)}, u32[]{:S(2)}) collective-permute-start(bf16[768,1152]{1,0:T(8,128)(2,1)} %param.24), channel_id=1, source_target_pairs={{0,1},{1,2},{2,3},{3,0},{4,5},{5,6},{6,7},{7,4},{8,9},{9,10},{10,1... | collective-permute-start | bytes 5308424 | tf_op jit(solution)/shard_map/ppermute | solution.py:23
  917.7 93.3 %collective-permute-start.1 = (bf16[768,1152]{1,0:T(8,128)(2,1)}, bf16[768,1152]{1,0:T(8,128)(2,1)}, u32[]{:S(2)}, u32[]{:S(2)}) collective-permute-start(bf16[768,1152]{1,0:T(8,128)(2,1)} %param.24), channel_id=1, source_target_pairs={{0,3},{1,0},{2,1},{3,2},{4,7},{5,4},{6,5},{7,6},{8,11},{9,8},{10,9... | collective-permute-start | bytes 5308424 | tf_op jit(solution)/shard_map/ppermute | solution.py:26
  968.5 82.2 %collective-permute-start.2 = (bf16[768,1152]{1,0:T(8,128)(2,1)}, bf16[768,1152]{1,0:T(8,128)(2,1)}, u32[]{:S(2)}, u32[]{:S(2)}) collective-permute-start(bf16[768,1152]{1,0:T(8,128)(2,1)} %collective-permute-done), channel_id=1, source_target_pairs={{0,1},{1,2},{2,3},{3,0},{4,5},{5,6},{6,7},{7,4},{8,9},{9,10},{10,1... | collective-permute-start | bytes 5308424 | tf_op jit(solution)/shard_map/ppermute | solution.py:23
  969.4 3.4 copy-start.10
  1895.2 4.1 copy-start.28
  1895.2 82.5 %copy-start.29 = (f32[192]{0:T(256)S(1)}, f32[192]{0:T(256)}, u32[]{:S(2)}) copy-start(f32[192]{0:T(256)} %get-tuple-element.487) | copy-start | bytes 2308
  1978.9 6.3 copy-start.23
  (3 other events, 3.1 us)
Sparse Core Ops, SparseCore 0:
  9.8 57.3 all-gather.6
  72.1 62.7 all-gather.10
  138.3 61.4 all-gather.8
  201.5 38.7 all-gather.12
  241.9 135.6 all-gather.14
  379.3 76.6 all-gather.16
  606.4 137.4 reduce-scatter.18
  750.0 136.3 reduce-scatter.20
  891.6 192.8 reduce-scatter.24
  1090.1 166.0 reduce-scatter.22
  1262.0 220.1 reduce-scatter.16
  1488.8 397.9 reduce-scatter.14
  1890.1 19.9 all-reduce.11
